TPU v7x, 32 devices: a whole 2x2x4 slice. The times are simulated.
32 devices in a mesh: blk: 8 (over z, x), pair: 4 (over y, core).
Axes of the slice: x: 2, y: 2, z: 4, core: 2. Of those that a mesh axis runs over, the one named last changes fastest.
Arguments:
- records: bfloat16 [8, 1024, 2048], P('blk', 'pair'), may hold values from -100 to 100
- offsets: int32 [2], replicated, may hold values from 1 to 7, as said below
- source_side: int32 [8, 2], P('blk'), may hold values from 0 to 1
Outputs:
- first_side: bfloat16 [8, 2, 32, 128, 128], P('blk', None, 'pair')
- second_side: bfloat16 [8, 2, 32, 128, 128], P('blk', None, 'pair')
Inputs may be any that keep to these rules, and one draw needn't show every extreme that they name: `offsets`: distinct and increasing; the last one is 7.
All inputs are finite; a program needn't handle non-finite values.
Results may differ from a plain program's by a relative error of at most 0.012.
Values may be sent and summed in bfloat16 or wider, within the bound.
No kernel may reach another device: no remote copies, remote signals or barrier semaphores. Data moves between devices by JAX's collectives and lax.ppermute only.
A program may use at most 128 MiB of HBM per device.

v0:
```python
import math

import jax
import jax.numpy as jnp
from jax import lax
from jax.sharding import PartitionSpec as P

BLOCK_CH = 128
BINS = 128
SAMPLES = 2048
FIRST_BIN = 4
LAGS = 32


def as_sent(value):
    return jax.tree.map(lambda a: a.astype(jnp.bfloat16) if a.dtype == jnp.float32 else a, value)


def shifted_2(value, axis, steps):
    count = lax.axis_size(axis)
    leading, last = (max(0, -steps), min(count, count - steps))
    return lax.ppermute(value, axis, [(source, source + steps) for source in range(leading, last)])


def fourier_table():
    sample_index = jnp.arange(SAMPLES, dtype=jnp.int32)
    bin_index = FIRST_BIN + jnp.arange(BINS, dtype=jnp.int32)
    phase_index = sample_index[:, None] * bin_index[None, :] % SAMPLES
    angles = 2.0 * math.pi / SAMPLES * phase_index.astype(jnp.float32)
    hann_taper = 0.5 - 0.5 * jnp.cos(2.0 * math.pi / SAMPLES * sample_index.astype(jnp.float32))
    return jnp.stack(
        (hann_taper[:, None] * jnp.cos(angles), -hann_taper[:, None] * jnp.sin(angles)), axis=-1
    )


def shift_ahead(distance):
    return lambda block: jax.tree.map(
        lambda part, own: part.astype(own.dtype), shifted_2(as_sent(block), "blk", -distance), block
    )


def local(records, offsets, source_side):
    seg_local = records.shape[0]
    local_blocks = records.shape[1] // BLOCK_CH
    table_full = fourier_table()
    table_high = lax.optimization_barrier(table_full.astype(jnp.bfloat16))
    table_low = (table_full - table_high.astype(jnp.float32)).astype(jnp.bfloat16)
    traces = records.reshape(seg_local, local_blocks, BLOCK_CH, SAMPLES)
    spectrum = jnp.einsum("sbcn,nfr->bfsrc", traces, table_high, preferred_element_type=jnp.float32)
    spectrum = spectrum + jnp.einsum(
        "sbcn,nfr->bfsrc", traces, table_low, preferred_element_type=jnp.float32
    )
    band_power = jnp.sum(spectrum * spectrum, axis=3)
    band_level = jnp.mean(band_power, axis=-1)
    whiten_scale = 1.0 / jnp.sqrt(band_level + 1e-05)
    whitened = (spectrum * whiten_scale[:, :, :, None, None]).astype(jnp.bfloat16)
    regrouped = lax.all_to_all(
        lax.all_to_all(whitened, "pair", split_axis=1, concat_axis=0, tiled=True),
        "blk",
        split_axis=0,
        concat_axis=2,
        tiled=True,
    )
    own_block = regrouped[0]
    bin_local = own_block.shape[0]
    seg_total = own_block.shape[1]
    offset_total = offsets.shape[0]
    group_size = lax.axis_size("blk")
    window_size = min(16, group_size)
    bit_total = window_size.bit_length() - 1
    ahead_list = [shift_ahead(distance) for distance in range(1, window_size)]
    partners = jnp.stack(
        [lax.switch(offsets[slot] - 1, ahead_list, own_block) for slot in range(offset_total)]
    )
    reverse_side = (source_side[0] == 1)[:, None, None, None, None]
    own_many = jnp.broadcast_to(own_block[None], partners.shape)
    source = jnp.where(reverse_side, partners, own_many)
    receiver = jnp.where(reverse_side, own_many, partners)
    left_side = source.reshape(offset_total, bin_local, 2 * seg_total, BLOCK_CH)
    rotated = jnp.stack((receiver[:, :, :, 1], -receiver[:, :, :, 0]), axis=3)
    right_side = jnp.stack((receiver, rotated), axis=4).reshape(
        offset_total, bin_local, 2 * seg_total, 2, BLOCK_CH
    )
    cross = jnp.einsum(
        "kfsc,kfsrd->kfrcd", left_side, right_side, preferred_element_type=jnp.float32
    )
    cross_rows = cross.reshape(offset_total, 2 * bin_local, BLOCK_CH * BLOCK_CH)
    pair_index = lax.axis_index("pair")
    lag_index = jnp.arange(LAGS, dtype=jnp.int32) - LAGS // 2
    bin_index = FIRST_BIN + pair_index * bin_local + jnp.arange(bin_local, dtype=jnp.int32)
    phase_index = lag_index[:, None] * bin_index[None, :] % SAMPLES
    angles = 2.0 * math.pi / SAMPLES * phase_index.astype(jnp.float32)
    normalizer = 1.0 / math.sqrt(seg_total * BINS)
    lag_table = (jnp.stack((jnp.cos(angles), -jnp.sin(angles)), axis=-1) * normalizer).reshape(
        LAGS, 2 * bin_local
    )
    summed = lax.psum_scatter(
        jnp.einsum(
            "lq,kqx->lkx",
            lag_table,
            cross_rows,
            precision=lax.Precision.HIGHEST,
            preferred_element_type=jnp.float32,
        ).astype(jnp.bfloat16),
        "pair",
        scatter_dimension=0,
        tiled=True,
    ).astype(jnp.float32)
    lag_local = summed.shape[0]
    first_local = (
        summed.astype(jnp.bfloat16)
        .transpose(1, 0, 2)
        .reshape(offset_total, lag_local, BLOCK_CH, BLOCK_CH)
    )
    returned = first_local
    for bit_number in range(bit_total):
        shifted = shifted_2(returned, "blk", 1 << bit_number)
        selected = (jnp.right_shift(offsets, bit_number) % 2 == 1)[:, None, None, None]
        returned = jnp.where(selected, shifted, returned)
    return (first_local[None], returned[None])


def solution(mesh):
    placed = (P("blk", "pair", None), P(), P("blk", None))
    return jax.shard_map(
        local,
        mesh=mesh,
        in_specs=placed,
        out_specs=(P("blk", None, "pair", None, None), P("blk", None, "pair", None, None)),
        check_vma=False,
    )
```

profile of v0, /device:TPU:25, one launch (start us, length us, event | category | flops | bytes accessed | tf_op | source)
XLA Modules:
  0.0 181.7 jit_solution(7638834543979147514)
XLA Ops:
  7.2 4.2 %cosine_multiply_fusion = (f32[2048,128,1]{1,0,2:T(8,128)S(1)}, f32[2048,128,1]{1,0,2:T(8,128)S(1)}) fusion(s32[128]{0:T(128)S(1)} %iota_add_fusion, f32[2048]{0:T(1024)S(1)} %get-tuple-element.57, f32[2048]{0:T(1024)S(1)} %get-tuple-element.58), kind=kLoop, calls=%fused_computation.18 | loop fusion | flops 4194304 | bytes 2114048 | tf_op jit(solution)/shard_map/mul | solution.py:32
  13.4 4.0 %all-to-all-start = ((bf16[2,128,1,2,128]{4,0,3,2,1:T(2,128)(2,1)}), bf16[2,128,1,2,128]{4,0,3,2,1:T(2,128)(2,1)S(1)}, u32[]{:S(2)}, u32[]{:S(2)}) async-start(bf16[2,128,1,2,128]{4,0,3,2,1:T(2,128)(2,1)} %copy.65), calls=%async_computation | async-start | bytes 262144 | tf_op jit(solution)/shard_map/all_to_all | solution.py:58
  17.6 3.4 %all-to-all-done = bf16[2,128,1,2,128]{4,0,3,2,1:T(2,128)(2,1)S(1)} async-done(((bf16[2,128,1,2,128]{4,0,3,2,1:T(2,128)(2,1)}), bf16[2,128,1,2,128]{4,0,3,2,1:T(2,128)(2,1)S(1)}, u32[]{:S(2)}, u32[]{:S(2)}) %all-to-all-start) | async-done | bytes 131104 | tf_op jit(solution)/shard_map/all_to_all | solution.py:58
  21.6 5.5 %all-to-all-start.1 = ((bf16[8,32,1,2,128]{4,1,3,2,0:T(8,128)(2,1)}), bf16[8,32,1,2,128]{4,1,3,2,0:T(8,128)(2,1)S(1)}, u32[]{:S(2)}, u32[]{:S(2)}) async-start(bf16[8,32,1,2,128]{4,1,3,2,0:T(8,128)(2,1)} %bitcast.15), calls=%async_computation.1 | async-start | bytes 262144 | tf_op jit(solution)/shard_map/all_to_all | solution.py:57
  29.0 1.6 all-to-all-done.1
  30.7 4.9 %conditional.2 = (bf16[32,8,2,128]{3,2,1,0:T(2,128)(2,1)}) conditional(s32[]{:T(128)} %bitcast.19, bf16[32,8,2,128]{3,2,1,0:T(2,128)(2,1)S(1)} %copy.69, bf16[32,8,2,128]{3,2,1,0:T(2,128)(2,1)S(1)} %copy.69, bf16[32,8,2,128]{3,2,1,0:T(2,128)(2,1)S(1)} %copy.69, bf16[32,8,2,128]{3,2,1,0:T(2,128)(2,1)S(1)} %copy.69, ...), branch_computations={%region_1.2_spmd, %region_2.3_spmd, %region_3.4_spmd, %region_4.5_... | conditional | bytes 524336 | solution.py:73
  30.7 3.6 %collective-permute-start.1 = (bf16[32,8,2,128]{3,2,1,0:T(2,128)(2,1)S(1)}, bf16[32,8,2,128]{3,2,1,0:T(2,128)(2,1)}, u32[]{:S(2)}, u32[]{:S(2)}) collective-permute-start(bf16[32,8,2,128]{3,2,1,0:T(2,128)(2,1)S(1)} %param.1), channel_id=1, source_target_pairs={{8,0},{12,4},{16,8},{20,12},{24,16},{28,20},{9,1},{13,5},{17,9},{2... | collective-permute-start | bytes 393224 | tf_op jit(solution)/shard_map/cond/branch_1_fun/ppermute | solution.py:22
  34.3 1.3 collective-permute-done.1
  35.6 1.3 conditional.3
  35.6 1.3 collective-permute-start.13
  37.0 1.4 broadcast_select_fusion
  40.6 5.5 %convolution_bitcast_fusion = f32[2,32,2,128,128]{3,4,2,1,0:T(8,128)} fusion(bf16[2,32,16,1,128]{4,2,3,1,0:T(8,128)(2,1)S(1)} %bitcast.79, bf16[2,32,16,1,128]{4,2,3,1,0:T(8,128)(2,1)S(1)} %maximum_select_fusion, bf16[1,32,16,128]{3,2,1,0:T(8,128)(2,1)} %bitcast.30, bf16[1,32,16,128]{3,2,1,0:T(8,128)(2,1)} %bitcast.29, ...), kind=kOutput, calls=%fused_computation.2 | convolution fusion | flops 67633152 | bytes 9306114 | tf_op jit(solution)/shard_map/kfsc,kfsrd->kfrcd/dot_general | solution.py:84
  46.1 8.9 %copy.85 = f32[2,32,2,128,128]{4,3,2,1,0:T(8,128)} copy(f32[2,32,2,128,128]{3,4,2,1,0:T(8,128)} %convolution_bitcast_fusion) | data formatting | bytes 16777216 | tf_op jit(solution)/shard_map/kfsc,kfsrd->kfrcd/transpose | solution.py:84
  55.0 9.4 %reshape.414 = f32[2,64,16384]{2,1,0:T(8,128)} reshape(f32[2,32,2,128,128]{4,3,2,1,0:T(8,128)} %copy.85) | data formatting | bytes 16777216 | tf_op jit(solution)/shard_map/reshape | solution.py:87
  64.4 6.4 %fusion = bf16[2,4,8,16384]{3,2,1,0:T(8,128)(2,1)S(1)} fusion(f32[32,64,1]{0,1,2:T(8,128)S(1)} %bitcast.81, f32[2,64,16384]{2,1,0:T(8,128)} %reshape.414), kind=kOutput, calls=%fused_computation.1 | convolution fusion | flops 806354944 | bytes 10493952 | tf_op jit(solution)/shard_map/lq,kqx->lkx/dot_general | solution.py:98
  70.9 1.5 copy.97
  72.4 42.0 %reduce-scatter.4.cloned.1.call-done = bf16[8,32768]{1,0:T(8,128)(2,1)} async-done(((bf16[32,32768]{1,0:T(8,128)(2,1)}), bf16[8,32768]{1,0:T(8,128)(2,1)}) %reduce-scatter.4.cloned.1.call-update) | async-done | bytes 524304
  114.4 1.2 copy.87
  115.6 3.1 %collective-permute-start.14 = (bf16[2,8,128,128]{3,2,1,0:T(8,128)(2,1)S(1)}, bf16[2,8,128,128]{3,2,1,0:T(8,128)(2,1)S(1)}, u32[]{:S(2)}, u32[]{:S(2)}) collective-permute-start(bf16[2,8,128,128]{3,2,1,0:T(8,128)(2,1)S(1)} %copy.87), channel_id=1, source_target_pairs={{0,4},{4,8},{8,12},{12,16},{16,20},{20,24},{24,28},{1,5},{5,9},{9,... | collective-permute-start | bytes 1572872 | tf_op jit(solution)/shard_map/ppermute | solution.py:22
  118.8 12.3 %collective-permute-done.14 = bf16[2,8,128,128]{3,2,1,0:T(8,128)(2,1)S(1)} collective-permute-done((bf16[2,8,128,128]{3,2,1,0:T(8,128)(2,1)S(1)}, bf16[2,8,128,128]{3,2,1,0:T(8,128)(2,1)S(1)}, u32[]{:S(2)}, u32[]{:S(2)}) %collective-permute-start.14) | collective-permute-done | bytes 524320 | tf_op jit(solution)/shard_map/ppermute | solution.py:22
  132.2 1.3 collective-permute-start.15
  133.5 12.4 %collective-permute-done.15 = bf16[2,8,128,128]{3,2,1,0:T(8,128)(2,1)S(1)} collective-permute-done((bf16[2,8,128,128]{3,2,1,0:T(8,128)(2,1)S(1)}, bf16[2,8,128,128]{3,2,1,0:T(8,128)(2,1)S(1)}, u32[]{:S(2)}, u32[]{:S(2)}) %collective-permute-start.15) | collective-permute-done | bytes 524320 | tf_op jit(solution)/shard_map/ppermute | solution.py:22
  146.0 1.3 collective-permute-start.16
  148.2 25.7 %collective-permute-done.16 = bf16[2,8,128,128]{3,2,1,0:T(8,128)(2,1)S(1)} collective-permute-done((bf16[2,8,128,128]{3,2,1,0:T(8,128)(2,1)S(1)}, bf16[2,8,128,128]{3,2,1,0:T(8,128)(2,1)S(1)}, u32[]{:S(2)}, u32[]{:S(2)}) %collective-permute-start.16) | collective-permute-done | bytes 524320 | tf_op jit(solution)/shard_map/ppermute | solution.py:22
  (37 shorter events, 8.9 us)
Async XLA Ops:
  7.2 4.4 %copy-start = (bf16[1,256,2048]{2,1,0:T(8,128)(2,1)S(1)}, bf16[1,256,2048]{2,1,0:T(8,128)(2,1)}, u32[]{:S(2)}) copy-start(bf16[1,256,2048]{2,1,0:T(8,128)(2,1)} %param.17) | copy-start | bytes 3145732
  11.6 15.5 %copy-start.2 = (s32[2]{0:T(128)S(1)}, s32[2]{0:T(128)}, u32[]{:S(2)}) copy-start(s32[2]{0:T(128)} %param.18) | copy-start | bytes 28
  11.6 17.4 %copy-start.3 = (s32[1,2]{1,0:T(1,128)S(1)}, s32[1,2]{1,0:T(1,128)}, u32[]{:S(2)}) copy-start(s32[1,2]{1,0:T(1,128)} %param.19) | copy-start | bytes 28
  13.4 7.5 %all-to-all-start = ((bf16[2,128,1,2,128]{4,0,3,2,1:T(2,128)(2,1)}), bf16[2,128,1,2,128]{4,0,3,2,1:T(2,128)(2,1)S(1)}, u32[]{:S(2)}, u32[]{:S(2)}) async-start(bf16[2,128,1,2,128]{4,0,3,2,1:T(2,128)(2,1)} %copy.65), calls=%async_computation | async-start | bytes 262144 | tf_op jit(solution)/shard_map/all_to_all | solution.py:58
  21.6 8.9 %all-to-all-start.1 = ((bf16[8,32,1,2,128]{4,1,3,2,0:T(8,128)(2,1)}), bf16[8,32,1,2,128]{4,1,3,2,0:T(8,128)(2,1)S(1)}, u32[]{:S(2)}, u32[]{:S(2)}) async-start(bf16[8,32,1,2,128]{4,1,3,2,0:T(8,128)(2,1)} %bitcast.15), calls=%async_computation.1 | async-start | bytes 262144 | tf_op jit(solution)/shard_map/all_to_all | solution.py:57
  27.1 87.3 %reduce-scatter.4.cloned.1.call-start = ((), (), s32[]{:S(2)}) async-start(), calls=%async_computation.3 | async-start | bytes 2621440
  30.7 4.9 %collective-permute-start.1 = (bf16[32,8,2,128]{3,2,1,0:T(2,128)(2,1)S(1)}, bf16[32,8,2,128]{3,2,1,0:T(2,128)(2,1)}, u32[]{:S(2)}, u32[]{:S(2)}) collective-permute-start(bf16[32,8,2,128]{3,2,1,0:T(2,128)(2,1)S(1)} %param.1), channel_id=1, source_target_pairs={{8,0},{12,4},{16,8},{20,12},{24,16},{28,20},{9,1},{13,5},{17,9},{2... | collective-permute-start | bytes 393224 | tf_op jit(solution)/shard_map/cond/branch_1_fun/ppermute | solution.py:22
  35.6 1.3 collective-permute-start.13
  114.4 32.9 %copy-start.1 = (bf16[8,32768]{1,0:T(8,128)(2,1)S(1)}, bf16[8,32768]{1,0:T(8,128)(2,1)}, u32[]{:S(2)}) copy-start(bf16[8,32768]{1,0:T(8,128)(2,1)} %reduce-scatter.4.cloned.1.call-done) | copy-start | bytes 1572868
  115.6 15.4 %collective-permute-start.14 = (bf16[2,8,128,128]{3,2,1,0:T(8,128)(2,1)S(1)}, bf16[2,8,128,128]{3,2,1,0:T(8,128)(2,1)S(1)}, u32[]{:S(2)}, u32[]{:S(2)}) collective-permute-start(bf16[2,8,128,128]{3,2,1,0:T(8,128)(2,1)S(1)} %copy.87), channel_id=1, source_target_pairs={{0,4},{4,8},{8,12},{12,16},{16,20},{20,24},{24,28},{1,5},{5,9},{9,... | collective-permute-start | bytes 1572872 | tf_op jit(solution)/shard_map/ppermute | solution.py:22
  132.2 13.7 %collective-permute-start.15 = (bf16[2,8,128,128]{3,2,1,0:T(8,128)(2,1)S(1)}, bf16[2,8,128,128]{3,2,1,0:T(8,128)(2,1)S(1)}, u32[]{:S(2)}, u32[]{:S(2)}) collective-permute-start(bf16[2,8,128,128]{3,2,1,0:T(8,128)(2,1)S(1)} %broadcast_select_fusion.1), channel_id=1, source_target_pairs={{0,8},{4,12},{8,16},{12,20},{16,24},{20,28},{1,9},{5,13},{9,17},{1... | collective-permute-start | bytes 1572872 | tf_op jit(solution)/shard_map/ppermute | solution.py:22
  146.0 27.9 %collective-permute-start.16 = (bf16[2,8,128,128]{3,2,1,0:T(8,128)(2,1)S(1)}, bf16[2,8,128,128]{3,2,1,0:T(8,128)(2,1)S(1)}, u32[]{:S(2)}, u32[]{:S(2)}) collective-permute-start(bf16[2,8,128,128]{3,2,1,0:T(8,128)(2,1)S(1)} %broadcast_select_fusion.2), channel_id=1, source_target_pairs={{0,16},{4,20},{8,24},{12,28},{1,17},{5,21},{9,25},{13,29},{2,18},{... | collective-permute-start | bytes 1572872 | tf_op jit(solution)/shard_map/ppermute | solution.py:22
Sparse Core Ops, SparseCore 0:
  72.5 41.8 reduce-scatter.3
where the time goes:
time: 183 us; the launch traced here: 182 us
  waiting for transfers between devices  98.6 us (54%)
  local copies, waits for them, and re-layouts  24.2 us (13%)
  starting transfers between devices  20 us (11%)
  between operations  15.4 us (8%)
  matrix products  12.9 us (7%)
  other arithmetic  10.4 us (6%)
    ppermute x5, waiting for transfers between devices, shifted_2(): lax.ppermute(value, axis, [(source, source + steps) for source in range(l...  51.6 us
    unnamed x2, waiting for transfers between devices  42 us
    ppermute x5, starting transfers between devices, shifted_2(): lax.ppermute(value, axis, [(source, source + steps) for source in range(l...  10.6 us
    reshape x1, local copies, waits for them, and re-layouts, local(): cross_rows = cross.reshape(offset_total, 2 * bin_local, BLOCK_CH * BLOCK_CH)  9.44 us
    transpose x1, local copies, waits for them, and re-layouts, local(): jnp.einsum('kfsc,kfsrd->kfrcd', left_side, right_side, preferred_element_...  8.89 us
    dot_general x1, matrix products, local(): jnp.einsum('lq,kqx->lkx', lag_table, cross_rows, precision=lax.Precision....  6.43 us
    dot_general x1, matrix products, local(): jnp.einsum('kfsc,kfsrd->kfrcd', left_side, right_side, preferred_element_...  5.54 us
    all_to_all x1, starting transfers between devices, local(): lax.all_to_all(lax.all_to_all(whitened, 'pair', split_axis=1, concat_axis...  5.46 us
  transfers between devices with their start and end apart: 8, of which 7 were waited for; matrix products, arithmetic and copies ran while one was open for 1% of the time, Pallas kernels for 0%

commit v1 on v0

v1 whole, which is shorter than its diff:
```python
import math

import jax
import jax.numpy as jnp
import numpy as np
from jax import lax
from jax.experimental import pallas as pl
from jax.experimental.pallas import tpu as pltpu
from jax.sharding import PartitionSpec as P

BLOCK_CH = 128
BINS = 128
SAMPLES = 2048
FIRST_BIN = 4
LAGS = 32
HALF_CH = BLOCK_CH // 2
BLOCKS_PER_STEP = 2
SEGS_PER_STEP = 8
FLAG_ROWS = 8
SLOT_ROWS = 2 * HALF_CH


def fourier_table():
    sample_index = np.arange(SAMPLES)
    bin_index = FIRST_BIN + np.arange(BINS)
    angles = 2.0 * math.pi / SAMPLES * (sample_index[:, None] * bin_index[None, :] % SAMPLES)
    hann_taper = 0.5 - 0.5 * np.cos(2.0 * math.pi / SAMPLES * sample_index)
    full = np.concatenate(
        (hann_taper[:, None] * np.cos(angles), -hann_taper[:, None] * np.sin(angles)), axis=1
    ).astype(np.float32)
    high = full.astype(jnp.bfloat16)
    low = (full - high.astype(np.float32)).astype(jnp.bfloat16)
    return np.concatenate((high, low), axis=1)


def lag_tables():
    lag_index = np.arange(LAGS) - LAGS // 2
    bin_index = FIRST_BIN + np.arange(BINS)
    angles = 2.0 * math.pi / SAMPLES * (lag_index[:, None] * bin_index[None, :] % SAMPLES)
    return np.cos(angles).astype(np.float32), np.sin(angles).astype(np.float32)


def whiten(records, half_of):
    blocks = records.shape[0] // BLOCK_CH
    step_blocks = min(BLOCKS_PER_STEP, blocks)

    def kernel(records_ref, table_ref, mine_ref, other_ref, held):
        half = half_of(lax.axis_index("pair"))
        both = jnp.dot(records_ref[...], table_ref[...], preferred_element_type=jnp.float32)
        spectrum = both[:, : 2 * BINS] + both[:, 2 * BINS :]
        for block in range(step_blocks):
            part = spectrum[block * BLOCK_CH : (block + 1) * BLOCK_CH]
            real, imag = part[:, :BINS], part[:, BINS:]
            level = jnp.mean(real * real + imag * imag, axis=0, keepdims=True)
            scale = 1.0 / jnp.sqrt(level + 1e-05)
            for index, value in enumerate((real * scale, imag * scale)):
                rounded = value.astype(jnp.bfloat16)
                held[block, 0, index] = rounded[:HALF_CH]
                held[block, 1, index] = rounded[HALF_CH:]
            mine_ref[block] = held[block, half]
            other_ref[block] = held[block, 1 - half]

    shape = (blocks, 2, HALF_CH, BINS)
    spec = pl.BlockSpec((step_blocks,) + shape[1:], lambda b: (b, 0, 0, 0))
    return pl.pallas_call(
        kernel,
        grid=(blocks // step_blocks,),
        in_specs=[
            pl.BlockSpec((step_blocks * BLOCK_CH, SAMPLES), lambda b: (b, 0)),
            pl.BlockSpec((SAMPLES, 4 * BINS), lambda b: (0, 0)),
        ],
        out_specs=[spec, spec],
        out_shape=[jax.ShapeDtypeStruct(shape, jnp.bfloat16)] * 2,
        scratch_shapes=[pltpu.VMEM((step_blocks, 2, 2, HALF_CH, BINS), jnp.bfloat16)],
        name="whiten",
    )(records, jnp.asarray(fourier_table()))


def partner_of(row, slot, offset_at, group, offset_total):
    if group_is_window(group) and offset_total == 2:
        last = group - 1
        if slot == 0:
            ahead = row + offset_at(0)
            return jnp.where(ahead < group, ahead, row - last)
        behind = row - offset_at(0)
        return jnp.where(behind >= 0, behind, row + last)
    step = offset_at(slot % offset_total)
    return row + step if slot < offset_total else row - step


def group_is_window(group):
    return group <= 16


def slot_total(group, offset_total):
    return 2 if group_is_window(group) and offset_total == 2 else 2 * offset_total


def slot_of(row, side, k, offset_at, group, offset_total):
    if group_is_window(group) and offset_total == 2:
        if k == 0:
            return side
        return jnp.where(row == 0, 1, 0)
    return side * offset_total + k


def pack(pieces, offsets, source_side, group):
    offset_total = offsets.shape[0]
    slots = slot_total(group, offset_total)
    piece_blocks = pieces[0].shape[0]
    rows = (1 + slots) * SLOT_ROWS

    def kernel(offsets_ref, side_ref, *refs):
        piece_refs, out_ref, held = refs[: len(pieces)], refs[-2], refs[-1]
        pair = lax.axis_index("pair")
        for turn, piece_ref in enumerate(piece_refs):
            first = (pair ^ turn) * piece_blocks
            for block in range(piece_blocks):
                held[first + block] = piece_ref[block].reshape(SLOT_ROWS, BINS)
        lane = lax.broadcasted_iota(jnp.int32, (FLAG_ROWS, BINS), 1)
        flags = jnp.zeros((FLAG_ROWS, BINS), jnp.float32)
        for k in range(offset_total):
            flags = jnp.where(lane == k, side_ref[0, k].astype(jnp.float32), flags)
        flags = flags.astype(jnp.bfloat16)

        def fill(row, carry):
            out_ref[row, :SLOT_ROWS] = held[row]
            for slot in range(slots):
                partner = partner_of(row, slot, lambda k: offsets_ref[k], group, offset_total)
                partner = jnp.clip(partner, 0, group - 1)
                out_ref[row, (slot + 1) * SLOT_ROWS : (slot + 2) * SLOT_ROWS] = held[partner]
            out_ref[row, rows:] = flags
            return carry

        lax.fori_loop(0, group, fill, 0)

    smem = pl.BlockSpec(memory_space=pltpu.SMEM)
    vmem = pl.BlockSpec(memory_space=pltpu.VMEM)
    return pl.pallas_call(
        kernel,
        in_specs=[smem, smem] + [vmem] * len(pieces),
        out_specs=vmem,
        out_shape=jax.ShapeDtypeStruct((group, rows + FLAG_ROWS, BINS), jnp.bfloat16),
        scratch_shapes=[pltpu.VMEM((group, SLOT_ROWS, BINS), jnp.bfloat16)],
        name="pack",
    )(offsets, source_side, *pieces)


def correlate(mine, theirs, offsets, source_side, group, lag_local, half_of):
    offset_total = offsets.shape[0]
    slots = slot_total(group, offset_total)
    segs = mine.shape[0]
    steps = segs // SEGS_PER_STEP
    depth = SEGS_PER_STEP * 2 * BINS
    normalizer = 1.0 / math.sqrt(segs * BINS)
    flag_row = (1 + slots) * SLOT_ROWS

    def kernel(
        offsets_ref, side_ref, flags_ref, cos_ref, sin_ref, mine_ref, theirs_ref,
        first_ref, second_ref, left, right, total,
    ):
        slab, step = pl.program_id(0), pl.program_id(1)
        row, pair = lax.axis_index("blk"), lax.axis_index("pair")
        half = half_of(pair)
        side, k = slab // offset_total, slab % offset_total
        other = jnp.where(side == 0, row + offsets_ref[k], row - offsets_ref[k])
        valid = jnp.logical_and(other >= 0, other < group)
        lane = lax.broadcasted_iota(jnp.int32, (FLAG_ROWS, BINS), 1)
        flag_seg = jnp.clip(other, 0, group - 1)
        far_flags = flags_ref[flag_seg].astype(jnp.float32)
        far_side = jnp.max(jnp.where(lane == k, far_flags, 0.0)) > 0.5
        swapped = jnp.where(side == 0, side_ref[0, k] == 1, jnp.logical_not(far_side))
        slot = 0
        for a_side in range(2):
            for a_k in range(offset_total):
                here = slot_of(row, a_side, a_k, lambda j: offsets_ref[j], group, offset_total)
                slot = jnp.where(slab == a_side * offset_total + a_k, here, slot)
        slot = slot + 1
        source = pl.multiple_of(jnp.where(swapped, slot, 0) * SLOT_ROWS, SLOT_ROWS)
        receiver = pl.multiple_of(jnp.where(swapped, 0, slot) * SLOT_ROWS, SLOT_ROWS)

        def emit(value):
            value = value.reshape(1, 1, lag_local, BLOCK_CH, BLOCK_CH)

            @pl.when(side == 0)
            def _():
                first_ref[...] = value

            @pl.when(side != 0)
            def _():
                second_ref[...] = value

        @pl.when(jnp.logical_not(valid))
        def _():
            emit(jnp.zeros((lag_local, BLOCK_CH, BLOCK_CH), jnp.bfloat16))

        @pl.when(valid)
        def _():
            lag_rows = pl.ds(pl.multiple_of(pair * lag_local, lag_local), lag_local)
            cosines, sines = cos_ref[lag_rows], sin_ref[lag_rows]
            for seg in range(SEGS_PER_STEP):
                at = seg * 2 * BINS
                for which, ref in ((half, mine_ref), (1 - half, theirs_ref)):
                    top = pl.multiple_of(which * HALF_CH, HALF_CH)
                    for part in range(2):
                        right[pl.ds(top, HALF_CH), at + part * BINS : at + (part + 1) * BINS] = ref[
                            seg, pl.ds(receiver + part * HALF_CH, HALF_CH)
                        ]
                    real = ref[seg, pl.ds(source, HALF_CH)].astype(jnp.float32)
                    imag = ref[seg, pl.ds(source + HALF_CH, HALF_CH)].astype(jnp.float32)
                    for lag in range(lag_local):
                        c, s = cosines[lag : lag + 1], sines[lag : lag + 1]
                        rows = pl.ds(lag * BLOCK_CH + top, HALF_CH)
                        left[rows, at : at + BINS] = (real * c + imag * s).astype(jnp.bfloat16)
                        left[rows, at + BINS : at + 2 * BINS] = (imag * c - real * s).astype(
                            jnp.bfloat16
                        )
            product = lax.dot_general(
                left[...], right[...], (((1,), (1,)), ((), ())), preferred_element_type=jnp.float32
            )
            if steps == 1:
                emit((product * normalizer).astype(jnp.bfloat16))
            else:

                @pl.when(step == 0)
                def _():
                    total[...] = product

                @pl.when(step > 0)
                def _():
                    total[...] += product

                @pl.when(step == steps - 1)
                def _():
                    emit((total[...] * normalizer).astype(jnp.bfloat16))

    smem = pl.BlockSpec(memory_space=pltpu.SMEM)
    vmem = pl.BlockSpec(memory_space=pltpu.VMEM)
    chunk = pl.BlockSpec((SEGS_PER_STEP,) + mine.shape[1:], lambda a, b: (b, 0, 0))
    out_shape = (1, offset_total, lag_local, BLOCK_CH, BLOCK_CH)
    out_block = (1, 1) + out_shape[2:]
    cos_table, sin_table = lag_tables()
    flag_block = flag_row // FLAG_ROWS
    return pl.pallas_call(
        kernel,
        grid=(2 * offset_total, steps),
        in_specs=[
            smem,
            smem,
            pl.BlockSpec((segs, FLAG_ROWS, BINS), lambda a, b: (0, flag_block, 0)),
            vmem,
            vmem,
            chunk,
            chunk,
        ],
        out_specs=[
            pl.BlockSpec(out_block, lambda a, b: (0, jnp.minimum(a, offset_total - 1), 0, 0, 0)),
            pl.BlockSpec(out_block, lambda a, b: (0, jnp.maximum(a - offset_total, 0), 0, 0, 0)),
        ],
        out_shape=[jax.ShapeDtypeStruct(out_shape, jnp.bfloat16)] * 2,
        scratch_shapes=[
            pltpu.VMEM((lag_local * BLOCK_CH, depth), jnp.bfloat16),
            pltpu.VMEM((BLOCK_CH, depth), jnp.bfloat16),
            pltpu.VMEM((lag_local * BLOCK_CH, BLOCK_CH), jnp.float32),
        ],
        name="correlate",
    )(offsets, source_side, mine, jnp.asarray(cos_table), jnp.asarray(sin_table), mine, theirs)


def local(records, offsets, source_side):
    group, pairs = lax.axis_size("blk"), lax.axis_size("pair")
    half_of = lambda pair: pair % 2
    assert records.shape[0] == 1
    swap = lambda value, turn: lax.ppermute(value, "pair", [(a, a ^ turn) for a in range(pairs)])
    mine, other = whiten(records.reshape(records.shape[0] * records.shape[1], SAMPLES), half_of)
    pieces = [mine] + [swap(other if turn % 2 else mine, turn) for turn in range(1, pairs)]
    packed = pack(pieces, offsets, source_side, group)
    arrived = lax.all_to_all(packed, "blk", split_axis=0, concat_axis=0, tiled=True)
    arrived_other = swap(arrived, 1)
    first, second = correlate(
        arrived, arrived_other, offsets, source_side, group, LAGS // pairs, half_of
    )
    return first, second


def solution(mesh):
    placed = (P("blk", "pair", None), P(), P("blk", None))
    return jax.shard_map(
        local,
        mesh=mesh,
        in_specs=placed,
        out_specs=(P("blk", None, "pair", None, None), P("blk", None, "pair", None, None)),
        check_vma=False,
    )
```

time: 183 us -> 53.6 us (0.29)
  the two profiles are of different devices: /device:TPU:25 before, /device:TPU:0 now
where the time goes in v1:
time: 53.6 us; the launch traced here: 53.3 us
  blocking collectives  27.1 us (51%)
  Pallas kernels  13.7 us (26%)
  waiting for transfers between devices  6.53 us (12%)
  starting transfers between devices  3.12 us (6%)
  local copies, waits for them, and re-layouts  2.17 us (4%)
  between operations  0.64 us (1%)
    all_to_all x1, blocking collectives, local(): lax.all_to_all(packed, 'blk', split_axis=0, concat_axis=0, tiled=True)  27.1 us
    pallas_call x1, Pallas kernels, correlate(): pl.pallas_call(kernel, grid=(2 * offset_total, steps), in_specs=[smem, sm...  8.45 us
    ppermute x4, waiting for transfers between devices, local(): lax.ppermute(value, 'pair', [(a, a ^ turn) for a in range(pairs)])  6.53 us
    pallas_call x1, Pallas kernels, whiten(): pl.pallas_call(kernel, grid=(blocks // step_blocks,), in_specs=[pl.BlockS...  3.34 us
    ppermute x4, starting transfers between devices, local(): lax.ppermute(value, 'pair', [(a, a ^ turn) for a in range(pairs)])  3.12 us
    unnamed x10, local copies, waits for them, and re-layouts  2.17 us
    pallas_call x1, Pallas kernels, pack(): pl.pallas_call(kernel, in_specs=[smem, smem] + [vmem] * len(pieces), out_...  1.95 us
  transfers between devices with their start and end apart: 4, of which 3 were waited for; matrix products, arithmetic and copies ran while one was open for 0% of the time, Pallas kernels for 0%

profile of v1, /device:TPU:0, one launch (start us, length us, event | category | flops | bytes accessed | tf_op | source)
XLA Modules:
  0.0 53.3 jit_solution(14412835994546056806)
XLA Ops:
  0.6 3.3 %whiten.1 = (bf16[2,2,64,128]{3,2,1,0:T(8,128)(2,1)}, bf16[2,2,64,128]{3,2,1,0:T(8,128)(2,1)}) custom-call(bf16[256,2048]{1,0:T(8,128)(2,1)} %bitcast.1, bf16[2048,512]{1,0:T(8,128)(2,1)} %constant.6.clone.table_ref), custom_call_target="tpu_custom_call" | custom-call | tf_op jit(solution)/shard_map/whiten/pallas_call | solution.py:65
  4.0 3.0 %collective-permute-start.1 = (bf16[2,2,64,128]{3,2,1,0:T(8,128)(2,1)}, bf16[2,2,64,128]{3,2,1,0:T(8,128)(2,1)S(1)}, u32[]{:S(2)}, u32[]{:S(2)}) collective-permute-start(bf16[2,2,64,128]{3,2,1,0:T(8,128)(2,1)} %get-tuple-element.4.refs_0_), channel_id=1, source_target_pairs={{0,2},{1,3},{2,0},{3,1},{4,6},{5,7},{6,4},{7,5},{8,10},{9,11},{10,... | collective-permute-start | bytes 196616 | tf_op jit(solution)/shard_map/ppermute | solution.py:274
  7.0 0.0 collective-permute-start.2
  7.0 0.1 collective-permute-start
  7.1 2.3 %collective-permute-done.1.refs_2_ = bf16[2,2,64,128]{3,2,1,0:T(8,128)(2,1)S(1)} collective-permute-done((bf16[2,2,64,128]{3,2,1,0:T(8,128)(2,1)}, bf16[2,2,64,128]{3,2,1,0:T(8,128)(2,1)S(1)}, u32[]{:S(2)}, u32[]{:S(2)}) %collective-permute-start.1) | collective-permute-done | bytes 65568 | tf_op jit(solution)/shard_map/ppermute | solution.py:274
  9.4 0.0 copy-start.2
  9.4 1.9 %collective-permute-done.2.refs_3_ = bf16[2,2,64,128]{3,2,1,0:T(8,128)(2,1)S(1)} collective-permute-done((bf16[2,2,64,128]{3,2,1,0:T(8,128)(2,1)}, bf16[2,2,64,128]{3,2,1,0:T(8,128)(2,1)S(1)}, u32[]{:S(2)}, u32[]{:S(2)}) %collective-permute-start.2) | collective-permute-done | bytes 65568 | tf_op jit(solution)/shard_map/ppermute | solution.py:274
  11.3 0.0 copy-start.3
  11.3 0.0 collective-permute-done.refs_1_
  11.3 0.0 copy-done.2
  11.3 0.6 %copy-done.3 = bf16[2,2,64,128]{3,2,1,0:T(8,128)(2,1)} copy-done((bf16[2,2,64,128]{3,2,1,0:T(8,128)(2,1)}, bf16[2,2,64,128]{3,2,1,0:T(8,128)(2,1)S(1)}, u32[]{:S(2)}) %copy-start.3) | copy-done | bytes 65560
  11.9 0.0 copy-start.4
  11.9 0.6 %copy-done.4 = bf16[2,2,64,128]{3,2,1,0:T(8,128)(2,1)} copy-done((bf16[2,2,64,128]{3,2,1,0:T(8,128)(2,1)}, bf16[2,2,64,128]{3,2,1,0:T(8,128)(2,1)S(1)}, u32[]{:S(2)}) %copy-start.4) | copy-done | bytes 65560
  12.6 2.0 %pack.1 = bf16[8,392,128]{2,1,0:T(8,128)(2,1)} custom-call(s32[2]{0:T(128)} %offsets_ref.3, s32[1,2]{1,0:T(1,128)} %side_ref.3, bf16[2,2,64,128]{3,2,1,0:T(8,128)(2,1)} %get-tuple-element.4.refs_0_, bf16[2,2,64,128]{3,2,1,0:T(8,128)(2,1)} %copy-done.4, bf16[2,2,64,128]{3,2,1,0:T(8,128)(2,1)} %copy-done.2, bf16[2,2,64,128]{3,2,1,0:T(8,128)(2,1)} %copy-done.3), custom_call_target="tpu_custom_call" | custom-call | tf_op jit(solution)/shard_map/pack/pallas_call | solution.py:139
  14.5 27.1 %all_to_all.5.flags_ref.mine_ref = bf16[8,392,128]{2,1,0:T(8,128)(2,1)S(1)} all-to-all(bf16[8,392,128]{2,1,0:T(8,128)(2,1)} %pack.1), channel_id=1, replica_groups=mesh['blk'=8,'pair'=4] {'blk'}, dimensions={0} | all-to-all | bytes 1605632 | tf_op jit(solution)/shard_map/all_to_all | solution.py:278
  41.7 0.0 copy-start
  41.7 0.0 collective-permute-start.3
  41.7 2.3 %collective-permute-done.3.theirs_ref = bf16[8,392,128]{2,1,0:T(8,128)(2,1)S(1)} collective-permute-done((bf16[8,392,128]{2,1,0:T(8,128)(2,1)S(1)}, bf16[8,392,128]{2,1,0:T(8,128)(2,1)S(1)}, u32[]{:S(2)}, u32[]{:S(2)}) %collective-permute-start.3) | collective-permute-done | bytes 802848 | tf_op jit(solution)/shard_map/ppermute | solution.py:274
  44.0 0.0 copy-done
  44.0 0.0 copy-start.1
  44.0 0.9 %copy-done.1 = bf16[8,392,128]{2,1,0:T(8,128)(2,1)} copy-done((bf16[8,392,128]{2,1,0:T(8,128)(2,1)}, bf16[8,392,128]{2,1,0:T(8,128)(2,1)S(1)}, u32[]{:S(2)}) %copy-start.1) | copy-done | bytes 802840
  44.9 8.4 %correlate.1 = (bf16[1,2,8,128,128]{4,3,2,1,0:T(8,128)(2,1)}, bf16[1,2,8,128,128]{4,3,2,1,0:T(8,128)(2,1)}) custom-call(s32[2]{0:T(128)} %offsets_ref.3, s32[1,2]{1,0:T(1,128)} %side_ref.3, bf16[8,392,128]{2,1,0:T(8,128)(2,1)} %copy-done, f32[32,128]{1,0:T(8,128)} %constant.7.clone.cos_ref, f32[32,128]{1,0:T(8,128)} %constant.8.clone.sin_ref, ...), custom_call_target="tpu_custom_call" | custom-call | tf_op jit(solution)/shard_map/correlate/pallas_call | solution.py:244
Async XLA Ops:
  4.0 5.4 %collective-permute-start.1 = (bf16[2,2,64,128]{3,2,1,0:T(8,128)(2,1)}, bf16[2,2,64,128]{3,2,1,0:T(8,128)(2,1)S(1)}, u32[]{:S(2)}, u32[]{:S(2)}) collective-permute-start(bf16[2,2,64,128]{3,2,1,0:T(8,128)(2,1)} %get-tuple-element.4.refs_0_), channel_id=1, source_target_pairs={{0,2},{1,3},{2,0},{3,1},{4,6},{5,7},{6,4},{7,5},{8,10},{9,11},{10,... | collective-permute-start | bytes 196616 | tf_op jit(solution)/shard_map/ppermute | solution.py:274
  7.0 4.3 %collective-permute-start.2 = (bf16[2,2,64,128]{3,2,1,0:T(8,128)(2,1)}, bf16[2,2,64,128]{3,2,1,0:T(8,128)(2,1)S(1)}, u32[]{:S(2)}, u32[]{:S(2)}) collective-permute-start(bf16[2,2,64,128]{3,2,1,0:T(8,128)(2,1)} %get-tuple-element.5), channel_id=1, source_target_pairs={{0,3},{1,2},{2,1},{3,0},{4,7},{5,6},{6,5},{7,4},{8,11},{9,10},{10,... | collective-permute-start | bytes 196616 | tf_op jit(solution)/shard_map/ppermute | solution.py:274
  7.0 4.3 %collective-permute-start = (bf16[2,2,64,128]{3,2,1,0:T(8,128)(2,1)}, bf16[2,2,64,128]{3,2,1,0:T(8,128)(2,1)S(1)}, u32[]{:S(2)}, u32[]{:S(2)}) collective-permute-start(bf16[2,2,64,128]{3,2,1,0:T(8,128)(2,1)} %get-tuple-element.5), channel_id=1, source_target_pairs={{0,1},{1,0},{2,3},{3,2},{4,5},{5,4},{6,7},{7,6},{8,9},{9,8},{10,11... | collective-permute-start | bytes 196616 | tf_op jit(solution)/shard_map/ppermute | solution.py:274
  9.4 1.9 %copy-start.2 = (bf16[2,2,64,128]{3,2,1,0:T(8,128)(2,1)}, bf16[2,2,64,128]{3,2,1,0:T(8,128)(2,1)S(1)}, u32[]{:S(2)}) copy-start(bf16[2,2,64,128]{3,2,1,0:T(8,128)(2,1)S(1)} %collective-permute-done.1.refs_2_) | copy-start | bytes 196612
  11.3 0.6 %copy-start.3 = (bf16[2,2,64,128]{3,2,1,0:T(8,128)(2,1)}, bf16[2,2,64,128]{3,2,1,0:T(8,128)(2,1)S(1)}, u32[]{:S(2)}) copy-start(bf16[2,2,64,128]{3,2,1,0:T(8,128)(2,1)S(1)} %collective-permute-done.2.refs_3_) | copy-start | bytes 196612
  11.9 0.6 %copy-start.4 = (bf16[2,2,64,128]{3,2,1,0:T(8,128)(2,1)}, bf16[2,2,64,128]{3,2,1,0:T(8,128)(2,1)S(1)}, u32[]{:S(2)}) copy-start(bf16[2,2,64,128]{3,2,1,0:T(8,128)(2,1)S(1)} %collective-permute-done.refs_1_) | copy-start | bytes 196612
  41.7 2.3 %copy-start = (bf16[8,392,128]{2,1,0:T(8,128)(2,1)}, bf16[8,392,128]{2,1,0:T(8,128)(2,1)S(1)}, u32[]{:S(2)}) copy-start(bf16[8,392,128]{2,1,0:T(8,128)(2,1)S(1)} %all_to_all.5.flags_ref.mine_ref) | copy-start | bytes 2408452
  41.7 2.3 %collective-permute-start.3 = (bf16[8,392,128]{2,1,0:T(8,128)(2,1)S(1)}, bf16[8,392,128]{2,1,0:T(8,128)(2,1)S(1)}, u32[]{:S(2)}, u32[]{:S(2)}) collective-permute-start(bf16[8,392,128]{2,1,0:T(8,128)(2,1)S(1)} %all_to_all.5.flags_ref.mine_ref), channel_id=1, source_target_pairs={{0,1},{1,0},{2,3},{3,2},{4,5},{5,4},{6,7},{7,6},{8,9},{9,8},{10,11... | collective-permute-start | bytes 2408456 | tf_op jit(solution)/shard_map/ppermute | solution.py:274
  44.0 0.9 %copy-start.1 = (bf16[8,392,128]{2,1,0:T(8,128)(2,1)}, bf16[8,392,128]{2,1,0:T(8,128)(2,1)S(1)}, u32[]{:S(2)}) copy-start(bf16[8,392,128]{2,1,0:T(8,128)(2,1)S(1)} %collective-permute-done.3.theirs_ref) | copy-start | bytes 2408452
